TPU v7x, 256 devices: a whole 4x4x8 slice. The times are simulated.
256 devices in a mesh: tm: 8 (over x_hi, y), gx: 32 (over z, x_lo, core).
Axes of the slice: x: 4 (x_hi: 2, x_lo: 2; x = x_hi * 2 + x_lo), y: 4, z: 8, core: 2. Of those that a mesh axis runs over, the one named last changes fastest.
Arguments:
- start_states: float32 [8, 512, 128, 128], P('tm', 'gx'), may hold values from -1.2 to 1.2
- mobility: float32 [512, 128, 128], P('gx'), may hold values from 0.25 to 1
Outputs:
- end_state: float32 [8, 512, 128, 128], P('tm', 'gx')
- next_start: float32 [8, 512, 128, 128], P('tm', 'gx')
All inputs are finite; a program needn't handle non-finite values.
Results may differ from a plain program's by a relative error of at most 0.0001.
Values sent between devices are 32-bit elements; how exact they have to be, the bound alone decides.
A program may use at most 128 MiB of HBM per device.

v0:
```python
import math

import jax
import jax.numpy as jnp
from jax import lax
from jax.sharding import PartitionSpec as P

KY = 64
KZ = 64
ITERS = 2


time_step = 0.05


def with_halo(cells, sides, width):
    for axis, dim in sides:
        count = lax.axis_size(axis)
        ends = count - 1
        head = lax.slice_in_dim(cells, 0, width, axis=dim)
        tail = lax.slice_in_dim(cells, cells.shape[dim] - width, cells.shape[dim], axis=dim)
        cells = jnp.concatenate(
            [
                lax.ppermute(tail, axis, [(i, (i + 1) % count) for i in range(ends)]),
                cells,
                lax.ppermute(head, axis, [((i + 1) % count, i) for i in range(ends)]),
            ],
            axis=dim,
        )
    return cells


def shifted(value, axis, steps):
    count = lax.axis_size(axis)
    initial, last = (max(0, -steps), min(count, count - steps))
    return lax.ppermute(value, axis, [(source, source + steps) for source in range(initial, last)])


def basis_value(node_times, source, point):
    total = 1.0
    for other in range(5):
        if other != source:
            total = total * (point - node_times[other]) / (node_times[source] - node_times[other])
    return total


def picard_table():
    root = math.sqrt(3.0 / 7.0)
    node_times = [0.0, (1.0 - root) / 2.0, 0.5, (1.0 + root) / 2.0, 1.0]
    gauss_points = [-math.sqrt(0.6), 0.0, math.sqrt(0.6)]
    gauss_weights = [5.0 / 9.0, 8.0 / 9.0, 5.0 / 9.0]
    picard_rows = []
    for target in range(1, 5):
        upper = node_times[target]
        row_values = []
        for source in range(5):
            integral = 0.0
            for point, weight in zip(gauss_points, gauss_weights):
                integral = integral + 0.5 * upper * weight * basis_value(
                    node_times, source, 0.5 * upper * (1.0 + point)
                )
            row_values.append(integral)
        picard_rows.append(row_values)
    return picard_rows


def dct_rows(count, kept):
    freq = jnp.arange(kept, dtype=jnp.float32)[:, None]
    place = jnp.arange(count, dtype=jnp.float32)[None, :]
    matrix = jnp.cos(jnp.pi * (place + 0.5) * freq / count) * jnp.sqrt(2.0 / count)
    return jnp.where(freq == 0, matrix * jnp.sqrt(0.5), matrix)


def analyse(values):
    low_y = dct_rows(values.shape[1], KY)
    low_z = dct_rows(values.shape[2], KZ)
    hp = lax.Precision.HIGHEST
    coeffs = jnp.einsum("ky,xyz->xkz", low_y, values, precision=hp)
    coeffs = jnp.einsum("xkz,lz->xkl", coeffs, low_z, precision=hp)
    return coeffs.reshape(values.shape[0], KY * KZ)


def synthesise(coeffs, width_y, width_z):
    low_y = dct_rows(width_y, KY)
    low_z = dct_rows(width_z, KZ)
    hp = lax.Precision.HIGHEST
    blocks = coeffs.reshape(coeffs.shape[0], KY, KZ)
    back = jnp.einsum("xkl,lz->xkz", blocks, low_z, precision=hp)
    return jnp.einsum("ky,xkz->xyz", low_y, back, precision=hp)


def evaluate(padded, mobility):
    padded = jnp.pad(padded, ((0, 0), (0, 0), (1, 1), (1, 1)))
    values = padded[:, 1:-1, 1:-1, 1:-1]
    laplace = padded[:, 2:, 1:-1, 1:-1] + padded[:, :-2, 1:-1, 1:-1]
    laplace = laplace + padded[:, 1:-1, 2:, 1:-1] + padded[:, 1:-1, :-2, 1:-1]
    laplace = laplace + padded[:, 1:-1, 1:-1, 2:] + padded[:, 1:-1, 1:-1, :-2] - 6.0 * values
    return mobility * (laplace + values - values * values * values)


def sweep(start_value, nodes, mobility, picard_rows):
    fields = jnp.concatenate([start_value[None], nodes], axis=0)
    padded = with_halo(fields, (("gx", 1),), 1)
    node_rates = evaluate(padded, mobility)
    updated = []
    for target in range(4):
        total = picard_rows[target][0] * node_rates[0]
        for source in range(1, 5):
            total = total + picard_rows[target][source] * node_rates[source]
        updated.append(start_value + time_step * total)
    return jnp.stack(updated, axis=0)


def forward(end_value, start_value, receive_mask):
    width_y = start_value.shape[1]
    width_z = start_value.shape[2]
    arrived = shifted(end_value, "tm", 1)
    change = synthesise(analyse(arrived - start_value), width_y, width_z)
    return start_value + receive_mask * change


def body(start_states, mobility):
    picard_rows = picard_table()
    receive_mask = (lax.axis_index("tm") > 0).astype(jnp.float32)
    start_value = start_states[0]
    nodes = jnp.broadcast_to(start_value[None], (4,) + start_value.shape)
    end_value = start_value
    for iteration in range(ITERS):
        if iteration == 0:
            nodes = sweep(start_value, nodes, mobility, picard_rows)
        else:
            nodes = sweep(start_value, nodes, mobility, picard_rows)
        end_value = nodes[3]
        start_value = forward(end_value, start_value, receive_mask)
    return (end_value[None], start_value[None])


def solution(mesh):
    placed = (P("tm", "gx", None, None), P("gx", None, None))
    return jax.shard_map(
        body,
        mesh=mesh,
        in_specs=placed,
        out_specs=(P("tm", "gx", None, None), P("tm", "gx", None, None)),
        check_vma=False,
    )
```

profile of v0, /device:TPU:103, one launch (start us, length us, event | category | flops | bytes accessed | tf_op | source)
XLA Modules:
  0.0 159.9 jit_solution(14298329000838370093)
XLA Ops:
  0.6 1.6 copy.4
  2.7 2.0 %copy-done.2 = f32[4,16,128,128]{2,3,1,0:T(8,128)} copy-done((f32[4,16,128,128]{2,3,1,0:T(8,128)}, f32[4,16,128,128]{2,3,1,0:T(8,128)S(1)}, u32[]{:S(2)}) %copy-start.2) | copy-done | bytes 4194328
  4.7 5.6 %collective-permute-start.1 = (f32[5,1,128,128]{2,3,1,0:T(8,128)S(1)}, f32[5,1,128,128]{2,3,1,0:T(8,128)S(1)}, u32[]{:S(2)}, u32[]{:S(2)}) collective-permute-start(f32[5,1,128,128]{2,3,1,0:T(8,128)S(1)} %get-tuple-element.8), channel_id=1, source_target_pairs={{0,1},{1,2},{2,3},{3,4},{4,5},{5,6},{6,7},{7,8},{8,9},{9,10},{10,1... | collective-permute-start | bytes 983048 | tf_op jit(solution)/shard_map/ppermute | solution.py:24
  10.3 1.9 %collective-permute-start = (f32[5,1,128,128]{2,3,1,0:T(8,128)S(1)}, f32[5,1,128,128]{2,3,1,0:T(8,128)S(1)}, u32[]{:S(2)}, u32[]{:S(2)}) collective-permute-start(f32[5,1,128,128]{2,3,1,0:T(8,128)S(1)} %get-tuple-element.9), channel_id=1, source_target_pairs={{1,0},{2,1},{3,2},{4,3},{5,4},{6,5},{7,6},{8,7},{9,8},{10,9},{11,1... | collective-permute-start | bytes 983048 | tf_op jit(solution)/shard_map/ppermute | solution.py:26
  12.2 1.6 copy.5
  14.3 6.5 %collective-permute-done = f32[5,1,128,128]{2,3,1,0:T(8,128)S(1)} collective-permute-done((f32[5,1,128,128]{2,3,1,0:T(8,128)S(1)}, f32[5,1,128,128]{2,3,1,0:T(8,128)S(1)}, u32[]{:S(2)}, u32[]{:S(2)}) %collective-permute-start) | collective-permute-done | bytes 327712 | tf_op jit(solution)/shard_map/ppermute | solution.py:26
  20.8 0.7 copy-done.7
  21.5 9.5 %select_maximum_fusion.2 = f32[5,18,130,130]{2,3,1,0:T(8,128)S(1)} fusion(f32[5,1,128,128]{2,3,1,0:T(8,128)S(1)} %collective-permute-done, f32[5,1,128,128]{2,3,1,0:T(8,128)S(1)} %collective-permute-done.1, f32[4,16,128,128]{2,3,1,0:T(8,128)} %copy-done.2, f32[1,16,128,128]{2,3,1,0:T(8,128)S(1)} %copy.4), kind=kLoop, calls=%fused_computation.6 | loop fusion | flops 27378000 | bytes 11982240 | tf_op jit(solution)/shard_map/concatenate | solution.py:22
  31.1 6.9 %fusion.11 = f32[5,16,128,128]{2,3,1,0:T(8,128)S(1)} fusion(f32[4,16,128,128]{2,3,1,0:T(8,128)S(1)} %copy-done.3, f32[1,16,128,128]{2,3,1,0:T(8,128)S(1)} %copy.4, f32[5,18,130,130]{2,3,1,0:T(8,128)S(1)} %select_maximum_fusion.2, f32[5,1,128,128]{2,3,1,0:T(8,128)} %copy-done.6, f32[5,1,128,128]{2,3,1,0:T(8,128)} %copy-done.7, f32[16,128,128]{1,2,0:T(8,128)S(1)} %copy.5), kind=kLoop, calls=%fused_computation.26 | loop fusion | flops 22282240 | bytes 33161216 | tf_op jit(solution)/shard_map/mul | solution.py:98
  38.0 2.3 %copy-done = f32[5,16,128,128]{2,3,1,0:T(8,128)} copy-done((f32[5,16,128,128]{2,3,1,0:T(8,128)}, f32[5,16,128,128]{2,3,1,0:T(8,128)S(1)}, u32[]{:S(2)}) %copy-start) | copy-done | bytes 5242904
  40.3 2.0 %bitcast_add_fusion = (f32[16,128,128]{1,2,0:T(8,128)}, f32[1,16,128,128]{2,3,1,0:T(8,128)}) fusion(f32[1,16,128,128]{2,3,1,0:T(8,128)S(1)} %copy.4, f32[5,16,128,128]{2,3,1,0:T(8,128)S(1)} %fusion.11), kind=kLoop, calls=%fused_computation.67 | loop fusion | flops 2883584 | bytes 8388608 | tf_op jit(solution)/shard_map/add | solution.py:110
  42.3 3.4 %collective-permute-start.2 = (f32[16,128,128]{1,2,0:T(8,128)}, f32[16,128,128]{1,2,0:T(8,128)S(1)}, u32[]{:S(2)}, u32[]{:S(2)}) collective-permute-start(f32[16,128,128]{1,2,0:T(8,128)} %get-tuple-element.4), channel_id=1, source_target_pairs={{0,32},{32,64},{64,96},{96,128},{128,160},{160,192},{192,224},{1,3... | collective-permute-start | bytes 3145736 | tf_op jit(solution)/shard_map/ppermute | solution.py:36
  45.7 23.4 %collective-permute-done.2 = f32[16,128,128]{1,2,0:T(8,128)S(1)} collective-permute-done((f32[16,128,128]{1,2,0:T(8,128)}, f32[16,128,128]{1,2,0:T(8,128)S(1)}, u32[]{:S(2)}, u32[]{:S(2)}) %collective-permute-start.2) | collective-permute-done | bytes 1048608 | tf_op jit(solution)/shard_map/ppermute | solution.py:36
  69.0 1.1 convolution_bitcast_fusion.1
  70.1 1.8 %fusion.41 = f32[16,64,64]{2,1,0:T(8,128)S(1)} fusion(f32[16,64,128]{1,2,0:T(8,128)S(1)} %convolution_bitcast_fusion.1, f32[128]{0:T(128)S(1)} %add_multiply_fusion.1, pred[64]{0:T(512)(128)(4,1)S(1)} %iota_compare_fusion.4), kind=kOutput, calls=%fused_computation.86 | convolution fusion | flops 100704256 | bytes 787008 | tf_op jit(solution)/shard_map/xkz,lz->xkl/dot_general | solution.py:79
  72.0 0.7 fusion.39
  72.7 1.9 %bitcast_dynamic-update-slice_fusion = (f32[5,16,128,128]{2,3,1,0:T(8,128)S(1)}, f32[16,128,128]{1,2,0:T(8,128)S(1)}) fusion(f32[16,64,128]{2,1,0:T(8,128)S(1)} %fusion.39, f32[128]{0:T(128)S(1)} %add_multiply_fusion.1, pred[64]{0:T(512)(128)(4,1)S(1)} %iota_compare_fusion.4, f32[]{:T(128)S(6)} %convert_element_type.6, f32[1,16,128,128]{2,3,1,0:T(8,128)S(1)} %copy.4), kind=kOutput, calls=%fused_computation.66 | convolution fusion | flops 201891840 | bytes 3670596 | tf_op jit(solution)/shard_map/ky,xkz->xyz/dot_general | solution.py:89
  77.3 6.1 %collective-permute-start.4 = (f32[5,1,128,128]{2,3,1,0:T(8,128)S(1)}, f32[5,1,128,128]{2,3,1,0:T(8,128)S(1)}, u32[]{:S(2)}, u32[]{:S(2)}) collective-permute-start(f32[5,1,128,128]{2,3,1,0:T(8,128)S(1)} %get-tuple-element.6), channel_id=1, source_target_pairs={{0,1},{1,2},{2,3},{3,4},{4,5},{5,6},{6,7},{7,8},{8,9},{9,10},{10,1... | collective-permute-start | bytes 983048 | tf_op jit(solution)/shard_map/ppermute | solution.py:24
  83.4 2.1 %collective-permute-start.3 = (f32[5,1,128,128]{2,3,1,0:T(8,128)S(1)}, f32[5,1,128,128]{2,3,1,0:T(8,128)S(1)}, u32[]{:S(2)}, u32[]{:S(2)}) collective-permute-start(f32[5,1,128,128]{2,3,1,0:T(8,128)S(1)} %get-tuple-element.7), channel_id=1, source_target_pairs={{1,0},{2,1},{3,2},{4,3},{5,4},{6,5},{7,6},{8,7},{9,8},{10,9},{11,1... | collective-permute-start | bytes 983048 | tf_op jit(solution)/shard_map/ppermute | solution.py:26
  85.5 1.8 %collective-permute-done.4 = f32[5,1,128,128]{2,3,1,0:T(8,128)S(1)} collective-permute-done((f32[5,1,128,128]{2,3,1,0:T(8,128)S(1)}, f32[5,1,128,128]{2,3,1,0:T(8,128)S(1)}, u32[]{:S(2)}, u32[]{:S(2)}) %collective-permute-start.4) | collective-permute-done | bytes 327712 | tf_op jit(solution)/shard_map/ppermute | solution.py:24
  87.4 6.5 %collective-permute-done.3 = f32[5,1,128,128]{2,3,1,0:T(8,128)S(1)} collective-permute-done((f32[5,1,128,128]{2,3,1,0:T(8,128)S(1)}, f32[5,1,128,128]{2,3,1,0:T(8,128)S(1)}, u32[]{:S(2)}, u32[]{:S(2)}) %collective-permute-start.3) | collective-permute-done | bytes 327712 | tf_op jit(solution)/shard_map/ppermute | solution.py:26
  93.9 9.3 %select_maximum_fusion = f32[5,18,130,130]{2,3,1,0:T(8,128)} fusion(f32[5,1,128,128]{2,3,1,0:T(8,128)S(1)} %collective-permute-done.3, f32[5,16,128,128]{2,3,1,0:T(8,128)S(1)} %add_dynamic-update-slice_fusion, f32[5,1,128,128]{2,3,1,0:T(8,128)S(1)} %collective-permute-done.4), kind=kLoop, calls=%fused_computation.4 | loop fusion | flops 22815000 | bytes 11982240 | tf_op jit(solution)/shard_map/concatenate | solution.py:22
  103.2 21.4 %fusion.8 = f32[5,16,128,128]{2,3,1,0:T(8,128)} fusion(f32[5,16,128,128]{2,3,1,0:T(8,128)} %copy-done.4, f32[5,18,130,130]{2,3,1,0:T(8,128)} %select_maximum_fusion, f32[5,1,128,128]{2,3,1,0:T(8,128)S(1)} %collective-permute-done.4, f32[5,1,128,128]{2,3,1,0:T(8,128)S(1)} %collective-permute-done.3, f32[16,128,128]{1,2,0:T(8,128)S(1)} %copy.5), kind=kLoop, calls=%fused_computation.23 | loop fusion | flops 18350080 | bytes 33161216 | tf_op jit(solution)/shard_map/mul | solution.py:98
  124.6 3.1 %fusion.24 = f32[16,128,128]{1,2,0:T(8,128)S(1)} fusion(f32[16,128,128]{1,2,0:T(8,128)S(1)} %get-tuple-element.11, f32[5,16,128,128]{2,3,1,0:T(8,128)} %fusion.8), kind=kLoop, calls=%fused_computation.58 | loop fusion | flops 2883584 | bytes 7340032 | tf_op jit(solution)/shard_map/add | solution.py:110
  127.7 2.2 %collective-permute-start.5 = (f32[16,128,128]{1,2,0:T(8,128)S(1)}, f32[16,128,128]{1,2,0:T(8,128)S(1)}, u32[]{:S(2)}, u32[]{:S(2)}) collective-permute-start(f32[16,128,128]{1,2,0:T(8,128)S(1)} %fusion.24), channel_id=1, source_target_pairs={{0,32},{32,64},{64,96},{96,128},{128,160},{160,192},{192,224},{1,3... | collective-permute-start | bytes 3145736 | tf_op jit(solution)/shard_map/ppermute | solution.py:36
  129.9 1.3 copy.11
  131.2 21.9 %collective-permute-done.5 = f32[16,128,128]{1,2,0:T(8,128)S(1)} collective-permute-done((f32[16,128,128]{1,2,0:T(8,128)S(1)}, f32[16,128,128]{1,2,0:T(8,128)S(1)}, u32[]{:S(2)}, u32[]{:S(2)}) %collective-permute-start.5) | collective-permute-done | bytes 1048608 | tf_op jit(solution)/shard_map/ppermute | solution.py:36
  153.1 1.1 convolution_bitcast_fusion
  154.2 1.8 %fusion.35 = f32[16,64,64]{2,1,0:T(8,128)S(1)} fusion(f32[16,64,128]{1,2,0:T(8,128)S(1)} %convolution_bitcast_fusion, f32[128]{0:T(128)S(1)} %add_multiply_fusion.1, pred[64]{0:T(512)(128)(4,1)S(1)} %iota_compare_fusion.4), kind=kOutput, calls=%fused_computation.80 | convolution fusion | flops 100704256 | bytes 787008 | tf_op jit(solution)/shard_map/xkz,lz->xkl/dot_general | solution.py:79
  156.0 0.7 fusion.33
  156.7 1.8 %fusion.18 = f32[1,16,128,128]{2,3,1,0:T(8,128)S(1)} fusion(f32[16,128,128]{1,2,0:T(8,128)S(1)} %get-tuple-element.11, f32[16,64,128]{2,1,0:T(8,128)S(1)} %fusion.33, f32[]{:T(128)S(6)} %convert_element_type.6, f32[128]{0:T(128)S(1)} %add_multiply_fusion.1, pred[64]{0:T(512)(128)(4,1)S(1)} %iota_compare_fusion.4), kind=kOutput, calls=%fused_computation.50 | convolution fusion | flops 201891840 | bytes 2622020 | tf_op jit(solution)/shard_map/ky,xkz->xyz/dot_general | solution.py:89
  158.6 1.3 copy.12
  (23 shorter events, 3.8 us)
Async XLA Ops:
  2.7 2.0 %copy-start.2 = (f32[4,16,128,128]{2,3,1,0:T(8,128)}, f32[4,16,128,128]{2,3,1,0:T(8,128)S(1)}, u32[]{:S(2)}) copy-start(f32[4,16,128,128]{2,3,1,0:T(8,128)S(1)} %broadcast_in_dim.72) | copy-start | bytes 12582916
  4.7 9.6 %collective-permute-start.1 = (f32[5,1,128,128]{2,3,1,0:T(8,128)S(1)}, f32[5,1,128,128]{2,3,1,0:T(8,128)S(1)}, u32[]{:S(2)}, u32[]{:S(2)}) collective-permute-start(f32[5,1,128,128]{2,3,1,0:T(8,128)S(1)} %get-tuple-element.8), channel_id=1, source_target_pairs={{0,1},{1,2},{2,3},{3,4},{4,5},{5,6},{6,7},{7,8},{8,9},{9,10},{10,1... | collective-permute-start | bytes 983048 | tf_op jit(solution)/shard_map/ppermute | solution.py:24
  10.3 10.5 %collective-permute-start = (f32[5,1,128,128]{2,3,1,0:T(8,128)S(1)}, f32[5,1,128,128]{2,3,1,0:T(8,128)S(1)}, u32[]{:S(2)}, u32[]{:S(2)}) collective-permute-start(f32[5,1,128,128]{2,3,1,0:T(8,128)S(1)} %get-tuple-element.9), channel_id=1, source_target_pairs={{1,0},{2,1},{3,2},{4,3},{5,4},{6,5},{7,6},{8,7},{9,8},{10,9},{11,1... | collective-permute-start | bytes 983048 | tf_op jit(solution)/shard_map/ppermute | solution.py:26
  13.8 17.3 %copy-start.3 = (f32[4,16,128,128]{2,3,1,0:T(8,128)S(1)}, f32[4,16,128,128]{2,3,1,0:T(8,128)}, u32[]{:S(2)}) copy-start(f32[4,16,128,128]{2,3,1,0:T(8,128)} %copy-done.2) | copy-start | bytes 12582916
  14.3 6.5 %copy-start.6 = (f32[5,1,128,128]{2,3,1,0:T(8,128)}, f32[5,1,128,128]{2,3,1,0:T(8,128)S(1)}, u32[]{:S(2)}) copy-start(f32[5,1,128,128]{2,3,1,0:T(8,128)S(1)} %collective-permute-done.1) | copy-start | bytes 983044
  20.8 0.7 copy-start.7
  38.0 2.3 %copy-start = (f32[5,16,128,128]{2,3,1,0:T(8,128)}, f32[5,16,128,128]{2,3,1,0:T(8,128)S(1)}, u32[]{:S(2)}) copy-start(f32[5,16,128,128]{2,3,1,0:T(8,128)S(1)} %fusion.11) | copy-start | bytes 15728644
  42.3 26.8 %collective-permute-start.2 = (f32[16,128,128]{1,2,0:T(8,128)}, f32[16,128,128]{1,2,0:T(8,128)S(1)}, u32[]{:S(2)}, u32[]{:S(2)}) collective-permute-start(f32[16,128,128]{1,2,0:T(8,128)} %get-tuple-element.4), channel_id=1, source_target_pairs={{0,32},{32,64},{64,96},{96,128},{128,160},{160,192},{192,224},{1,3... | collective-permute-start | bytes 3145736 | tf_op jit(solution)/shard_map/ppermute | solution.py:36
  45.6 28.9 %copy-start.1 = (f32[5,16,128,128]{2,3,1,0:T(8,128)S(1)}, f32[5,16,128,128]{2,3,1,0:T(8,128)}, u32[]{:S(2)}) copy-start(f32[5,16,128,128]{2,3,1,0:T(8,128)} %copy-done) | copy-start | bytes 15728644
  75.9 1.2 copy-start.5
  77.2 16.7 %copy-start.4 = (f32[5,16,128,128]{2,3,1,0:T(8,128)}, f32[5,16,128,128]{2,3,1,0:T(8,128)S(1)}, u32[]{:S(2)}) copy-start(f32[5,16,128,128]{2,3,1,0:T(8,128)S(1)} %add_dynamic-update-slice_fusion) | copy-start | bytes 15728644
  77.3 10.1 %collective-permute-start.4 = (f32[5,1,128,128]{2,3,1,0:T(8,128)S(1)}, f32[5,1,128,128]{2,3,1,0:T(8,128)S(1)}, u32[]{:S(2)}, u32[]{:S(2)}) collective-permute-start(f32[5,1,128,128]{2,3,1,0:T(8,128)S(1)} %get-tuple-element.6), channel_id=1, source_target_pairs={{0,1},{1,2},{2,3},{3,4},{4,5},{5,6},{6,7},{7,8},{8,9},{9,10},{10,1... | collective-permute-start | bytes 983048 | tf_op jit(solution)/shard_map/ppermute | solution.py:24
  83.4 10.5 %collective-permute-start.3 = (f32[5,1,128,128]{2,3,1,0:T(8,128)S(1)}, f32[5,1,128,128]{2,3,1,0:T(8,128)S(1)}, u32[]{:S(2)}, u32[]{:S(2)}) collective-permute-start(f32[5,1,128,128]{2,3,1,0:T(8,128)S(1)} %get-tuple-element.7), channel_id=1, source_target_pairs={{1,0},{2,1},{3,2},{4,3},{5,4},{6,5},{7,6},{8,7},{9,8},{10,9},{11,1... | collective-permute-start | bytes 983048 | tf_op jit(solution)/shard_map/ppermute | solution.py:26
  127.7 25.4 %collective-permute-start.5 = (f32[16,128,128]{1,2,0:T(8,128)S(1)}, f32[16,128,128]{1,2,0:T(8,128)S(1)}, u32[]{:S(2)}, u32[]{:S(2)}) collective-permute-start(f32[16,128,128]{1,2,0:T(8,128)S(1)} %fusion.24), channel_id=1, source_target_pairs={{0,32},{32,64},{64,96},{96,128},{128,160},{160,192},{192,224},{1,3... | collective-permute-start | bytes 3145736 | tf_op jit(solution)/shard_map/ppermute | solution.py:36
where the time goes:
time: 163 us; the launch traced here: 160 us
  waiting for transfers between devices  60.6 us (37%)
  other arithmetic  54.4 us (33%)
  starting transfers between devices  21.3 us (13%)
  local copies, waits for them, and re-layouts  11.8 us (7%)
  matrix products  10.9 us (7%)
    ppermute x2, waiting for transfers between devices, shifted(): lax.ppermute(value, axis, [(source, source + steps) for source in range(i...  45.2 us
    mul x2, other arithmetic, evaluate(): return mobility * (laplace + values - values * values * values)  28.2 us
    concatenate x2, other arithmetic, with_halo(): jnp.concatenate([lax.ppermute(tail, axis, [(i, (i + 1) % count) for i in...  18.9 us
    ppermute x2, waiting for transfers between devices, with_halo(): lax.ppermute(head, axis, [((i + 1) % count, i) for i in range(ends)])  13 us
    ppermute x2, starting transfers between devices, with_halo(): lax.ppermute(tail, axis, [(i, (i + 1) % count) for i in range(ends)])  11.7 us
    unnamed x20, local copies, waits for them, and re-layouts  11.3 us
    ppermute x2, starting transfers between devices, shifted(): lax.ppermute(value, axis, [(source, source + steps) for source in range(i...  5.55 us
    add x2, other arithmetic, sweep(): updated.append(start_value + time_step * total)  5.12 us
  transfers between devices with their start and end apart: 6, of which 6 were waited for; matrix products, arithmetic and copies ran while one was open for 2% of the time, Pallas kernels for 0%

commit v1 on v0

v1 whole, which is shorter than its diff:
```python
import functools
import math

import jax
import jax.numpy as jnp
import ml_dtypes
import numpy as np
from jax import lax
from jax.experimental import pallas as pl
from jax.experimental.pallas import tpu as pltpu
from jax.sharding import PartitionSpec as P

KY = 64
KZ = 64
NY = 128
NZ = 128
time_step = 0.05
MESH = pl.DeviceIdType.MESH

FIRST = (1, 0, 3, 2)
SECOND = ((1, 2, 3, 4), (7, 8, 9, 10), (11, 12, 13, 14), (5, 6, 0, 15))


def basis_value(node_times, source, point):
    total = 1.0
    for other in range(5):
        if other != source:
            total = total * (point - node_times[other]) / (node_times[source] - node_times[other])
    return total


def picard_table():
    root = math.sqrt(3.0 / 7.0)
    node_times = [0.0, (1.0 - root) / 2.0, 0.5, (1.0 + root) / 2.0, 1.0]
    gauss_points = [-math.sqrt(0.6), 0.0, math.sqrt(0.6)]
    gauss_weights = [5.0 / 9.0, 8.0 / 9.0, 5.0 / 9.0]
    picard_rows = []
    for target in range(1, 5):
        upper = node_times[target]
        row_values = []
        for source in range(5):
            integral = 0.0
            for point, weight in zip(gauss_points, gauss_weights):
                integral = integral + 0.5 * upper * weight * basis_value(
                    node_times, source, 0.5 * upper * (1.0 + point)
                )
            row_values.append(integral)
        picard_rows.append(row_values)
    return picard_rows


def sweep_weights():
    rows = picard_table()
    last = rows[3]
    reach = [time_step * sum(row) for row in rows]
    moments = [sum(last[j] * reach[j - 1] ** k for j in range(1, 5)) for k in range(4)]
    return reach[3], last[0], moments


def dct_rows(count, kept):
    freq = np.arange(kept, dtype=np.float64)[:, None]
    place = np.arange(count, dtype=np.float64)[None, :]
    matrix = np.cos(np.pi * (place + 0.5) * freq / count) * np.sqrt(2.0 / count)
    return np.where(freq == 0, matrix * np.sqrt(0.5), matrix)


def two_parts(matrix):
    high = matrix.astype(ml_dtypes.bfloat16)
    low = (matrix - high.astype(np.float64)).astype(ml_dtypes.bfloat16)
    return high, low


def on_diagonal(block):
    zero = np.zeros_like(block)
    return np.block([[block, zero], [zero, block]])


LA, BA, DS, LS, PY, PZ, ROWS = 0, 128, 384, 768, 896, 1152, 1408


def tables():
    cy, cz = dct_rows(NY, KY), dct_rows(NZ, KZ)
    yh, yl = two_parts(cy)
    zh, zl = two_parts(cz)
    pyh, pyl = two_parts(cy.T @ cy)
    pzh, pzl = two_parts(cz.T @ cz)
    dh, dl = on_diagonal(zh), on_diagonal(zl)
    parts = [
        np.block([[yh, yh], [yl, yl]]),
        np.concatenate([dh.T, dl.T], axis=1),
        np.concatenate([dh, dh, dl], axis=0),
        np.concatenate([yh.T, yh.T, yl.T, yl.T], axis=1),
        np.block([[pyh, pyh], [pyl, pyl]]),
        np.block([[pzh, pzl], [pzh, pzl]]),
    ]
    return np.concatenate(parts, axis=0).astype(ml_dtypes.bfloat16)


def halves(value):
    high = value.astype(jnp.bfloat16)
    low = (value - high.astype(jnp.float32)).astype(jnp.bfloat16)
    return high, low


def mul(left, right):
    return jnp.dot(left, right, preferred_element_type=jnp.float32)


def analyse_pair(first, second, tab):
    high, low = halves(jnp.concatenate([first, second], axis=1))
    out = mul(tab[LA : LA + 128, :], jnp.concatenate([high, low], axis=0))
    return out[:64] + out[64:]


def analyse(planes, tab):
    rows = jnp.concatenate(
        [analyse_pair(planes[0], planes[1], tab), analyse_pair(planes[2], planes[3], tab)], axis=0
    )
    high, low = halves(rows)
    out = mul(jnp.concatenate([high, low], axis=0), tab[BA : BA + 256, :])
    return (out[:128, :128] + out[128:, :128]) + (out[:128, 128:] + out[128:, 128:])


def synthesise(block, tab):
    high, low = halves(block)
    rows = mul(jnp.concatenate([high, low, high], axis=1), tab[DS : DS + 384, :])
    planes = []
    for pair in range(2):
        high, low = halves(rows[64 * pair : 64 * pair + 64])
        out = mul(tab[LS : LS + 128, :], jnp.concatenate([high, low, high, low], axis=0))
        planes += [out[:, :128], out[:, 128:]]
    return planes


def smooth_pair(first, second, tab):
    high, low = halves(jnp.concatenate([first, second], axis=1))
    out = mul(tab[PY : PY + 256, :], jnp.concatenate([high, low], axis=0))
    out = out[:128] + out[128:]
    high, low = halves(jnp.concatenate([out[:, :128], out[:, 128:]], axis=0))
    out = mul(jnp.concatenate([high, low], axis=1), tab[PZ : PZ + 256, :])
    out = out[:, :128] + out[:, 128:]
    return out[:128], out[128:]


def kernel(
    a_hbm, mob_hbm, tab_hbm, end_hbm, next_hbm,
    a_v, mob_v, tab, f_v, w_v, r_v, ap_v, e_v, n_v, e1_v, cs, cr,
    in_sem, out_sem, ss, rs, hs, hr,
):
    t = lax.axis_index("tm")
    g = lax.axis_index("gx")
    g_count = lax.axis_size("gx")
    t_count = lax.axis_size("tm")
    has_left, has_right = g > 0, g < g_count - 1
    has_prev, has_next = t > 0, t < t_count - 1
    reach, q0, (s0, s1, s2, s3) = sweep_weights()

    loads = []
    for k, c in enumerate((0, 1, 2, 3)):
        loads.append(pltpu.make_async_copy(a_hbm.at[0, pl.ds(4 * c, 4)], a_v.at[pl.ds(1 + 4 * c, 4)], in_sem.at[c]))
    mob_loads = [
        pltpu.make_async_copy(mob_hbm.at[pl.ds(4 * c, 4)], mob_v.at[pl.ds(4 * c, 4)], in_sem.at[4 + c])
        for c in range(4)
    ]
    tab_loads = [
        pltpu.make_async_copy(tab_hbm.at[pl.ds(0, DS)], tab.at[pl.ds(0, DS)], in_sem.at[8]),
        pltpu.make_async_copy(tab_hbm.at[pl.ds(DS, ROWS - DS)], tab.at[pl.ds(DS, ROWS - DS)], in_sem.at[9]),
    ]
    for copy in (loads[0], loads[1], loads[2], mob_loads[1], loads[3], tab_loads[0], mob_loads[0], mob_loads[3], mob_loads[2], tab_loads[1]):
        copy.start()

    barrier = pltpu.get_barrier_semaphore()
    for present, axis, index in (
        (has_left, "gx", g - 1), (has_right, "gx", g + 1), (has_prev, "tm", t - 1), (has_next, "tm", t + 1),
    ):
        @pl.when(present)
        def _():
            pl.semaphore_signal(barrier, inc=1, device_id={axis: index}, device_id_type=MESH)

    zero = jnp.zeros((128, 128), jnp.float32)

    @pl.when(g == 0)
    def _():
        a_v[0] = zero
        w_v[0] = zero

    @pl.when(g == g_count - 1)
    def _():
        a_v[17] = zero
        w_v[17] = zero

    @pl.when(t == 0)
    def _():
        for stage in range(2):
            for c in range(4):
                cr[stage, c] = zero

    row = lax.broadcasted_iota(jnp.int32, (128, 128), 0)
    lane = lax.broadcasted_iota(jnp.int32, (128, 128), 1)

    def neighbours(ref, p):
        v = ref[p + 1]
        total = ref[p] + ref[p + 2]
        total = total + jnp.where(row == 0, 0.0, pltpu.roll(v, 1, 0))
        total = total + jnp.where(row == 127, 0.0, pltpu.roll(v, 127, 0))
        total = total + jnp.where(lane == 0, 0.0, pltpu.roll(v, 1, 1))
        total = total + jnp.where(lane == 127, 0.0, pltpu.roll(v, 127, 1))
        return total, v

    def first_rates(c):
        def step(i, carry):
            p = 4 * c + i
            total, v = neighbours(a_v, p)
            rate = mob_v[p] * (total - v * (5.0 + v * v))
            f_v[p] = rate
            e1_v[i] = v + reach * rate
            return carry

        lax.fori_loop(0, 4, step, 0)

    def send(stage, k):
        return pltpu.make_async_remote_copy(
            src_ref=cs.at[stage, k], dst_ref=cr.at[stage, k], send_sem=ss.at[stage, k], recv_sem=rs.at[stage, k],
            device_id={"tm": t + 1}, device_id_type=MESH,
        )

    def halo(ref, stage, side):
        return pltpu.make_async_remote_copy(
            src_ref=ref.at[1 if side == 0 else 16], dst_ref=ref.at[17 if side == 0 else 0],
            send_sem=hs.at[stage, side], recv_sem=hr.at[stage, side],
            device_id={"gx": g - 1 if side == 0 else g + 1}, device_id_type=MESH,
        )

    def start_halo(ref, stage, side):
        @pl.when(has_left if side == 0 else has_right)
        def _():
            halo(ref, stage, side).start()

    def take_halo(ref, stage, side):
        @pl.when(has_right if side == 0 else has_left)
        def _():
            halo(ref, stage, side).wait_recv()

    def forward(stage, k, planes):
        cs[stage, k] = analyse(planes, tab)

        @pl.when(has_next)
        def _():
            send(stage, k).start()

    def arrive(stage, k):
        @pl.when(has_prev)
        def _():
            send(stage, k).wait_recv()

    for c in range(4):
        loads[c].wait()
    mob_loads[1].wait()
    first_rates(1)
    pl.semaphore_wait(
        barrier,
        has_left.astype(jnp.int32) + has_right.astype(jnp.int32) + has_prev.astype(jnp.int32) + has_next.astype(jnp.int32),
    )
    start_halo(a_v, 0, 0)
    start_halo(a_v, 0, 1)
    tab_loads[0].wait()
    forward(0, 1, [e1_v[i] for i in range(4)])
    mob_loads[0].wait()
    take_halo(a_v, 0, 1)
    first_rates(0)
    forward(0, 0, [e1_v[i] for i in range(4)])
    mob_loads[3].wait()
    take_halo(a_v, 0, 0)
    first_rates(3)
    forward(0, 3, [e1_v[i] for i in range(4)])
    mob_loads[2].wait()
    first_rates(2)
    forward(0, 2, [e1_v[i] for i in range(4)])

    tab_loads[1].wait()
    receives = has_prev.astype(jnp.float32)

    def rest(i, carry):
        p = 2 * i
        first, second = a_v[p + 1], a_v[p + 2]
        low_first, low_second = smooth_pair(first, second, tab)
        r_v[p] = first - receives * low_first
        r_v[p + 1] = second - receives * low_second
        return carry

    lax.fori_loop(0, 8, rest, 0)

    def corrected(c):
        arrive(0, c)
        for i, plane in enumerate(synthesise(cr[0, c], tab)):
            p = 4 * c + i
            start = r_v[p] + plane
            ap_v[p] = start
            w_v[p + 1] = q0 * start + s0 * a_v[p + 1] + s1 * f_v[p]

    def second_values(low, count):
        def step(i, carry):
            p = low + i
            total, w = neighbours(w_v, p)
            a, f, start = a_v[p + 1], f_v[p], ap_v[p]
            square = a * a
            cubes = (s3 * f + (3.0 * s2) * a) * f + (3.0 * s1) * square
            cubes = cubes * f + s0 * (square * a) + q0 * (start * start * start)
            e_v[p] = start + (time_step * mob_v[p]) * ((total - 5.0 * w) - cubes)
            return carry

        lax.fori_loop(0, count, step, 0)

    def store_end(low, count, k):
        return pltpu.make_async_copy(e_v.at[pl.ds(low, count)], end_hbm.at[0, pl.ds(low, count)], out_sem.at[k])

    corrected(1)
    corrected(0)
    start_halo(w_v, 1, 0)
    second_values(1, 6)
    forward(1, 0, [e_v[p] for p in SECOND[0]])
    corrected(3)
    start_halo(w_v, 1, 1)
    corrected(2)
    second_values(7, 4)
    forward(1, 1, [e_v[p] for p in SECOND[1]])
    second_values(11, 4)
    forward(1, 2, [e_v[p] for p in SECOND[2]])
    take_halo(w_v, 1, 1)
    second_values(0, 1)
    take_halo(w_v, 1, 0)
    second_values(15, 1)
    forward(1, 3, [e_v[p] for p in SECOND[3]])
    store_end(0, 16, 0).start()

    def store_next(low, count, k):
        return pltpu.make_async_copy(n_v.at[pl.ds(low, count)], next_hbm.at[0, pl.ds(low, count)], out_sem.at[k])

    stores = [store_end(0, 16, 0)]
    pieces = (((1, 4),), ((7, 4),), ((11, 4),), ((5, 2), (0, 1), (15, 1)))
    for k in range(4):
        arrive(1, k)
        for p, plane in zip(SECOND[k], synthesise(cr[1, k], tab)):
            n_v[p] = r_v[p] + plane
        for low, count in pieces[k]:
            stores.append(store_next(low, count, len(stores)))
            stores[-1].start()

    for stage in range(2):
        @pl.when(has_next)
        def _():
            for k in range(4):
                send(stage, k).wait_send()

        ref = (a_v, w_v)[stage]

        @pl.when(has_left)
        def _():
            halo(ref, stage, 0).wait_send()

        @pl.when(has_right)
        def _():
            halo(ref, stage, 1).wait_send()
    for copy in stores:
        copy.wait()


def body(start_states, mobility):
    plane = (128, 128)
    f32 = jnp.float32
    out = jax.ShapeDtypeStruct(start_states.shape, f32)
    return pl.pallas_call(
        kernel,
        out_shape=(out, out),
        in_specs=[pl.BlockSpec(memory_space=pl.ANY)] * 3,
        out_specs=[pl.BlockSpec(memory_space=pl.ANY)] * 2,
        scratch_shapes=[
            pltpu.VMEM((18,) + plane, f32),
            pltpu.VMEM((16,) + plane, f32),
            pltpu.VMEM((ROWS, 256), jnp.bfloat16),
            pltpu.VMEM((16,) + plane, f32),
            pltpu.VMEM((18,) + plane, f32),
            pltpu.VMEM((16,) + plane, f32),
            pltpu.VMEM((16,) + plane, f32),
            pltpu.VMEM((16,) + plane, f32),
            pltpu.VMEM((16,) + plane, f32),
            pltpu.VMEM((4,) + plane, f32),
            pltpu.VMEM((2, 4) + plane, f32),
            pltpu.VMEM((2, 4) + plane, f32),
            pltpu.SemaphoreType.DMA((10,)),
            pltpu.SemaphoreType.DMA((8,)),
            pltpu.SemaphoreType.DMA((2, 4)),
            pltpu.SemaphoreType.DMA((2, 4)),
            pltpu.SemaphoreType.DMA((2, 2)),
            pltpu.SemaphoreType.DMA((2, 2)),
        ],
        compiler_params=pltpu.CompilerParams(
            collective_id=0, has_side_effects=True, vmem_limit_bytes=24 * 1024 * 1024
        ),
    )(start_states, mobility, jnp.asarray(tables()))


def solution(mesh):
    placed = (P("tm", "gx", None, None), P("gx", None, None))
    return jax.shard_map(
        body,
        mesh=mesh,
        in_specs=placed,
        out_specs=(P("tm", "gx", None, None), P("tm", "gx", None, None)),
        check_vma=False,
    )
```

time: 163 us -> 32.1 us (0.20)
  the two profiles are of different devices: /device:TPU:103 before, /device:TPU:6 now
where the time goes in v1:
time: 32.1 us; the launch traced here: 31.9 us
  Pallas kernels  25.8 us (80%)
  local copies, waits for them, and re-layouts  5.49 us (17%)
  between operations  0.65 us (2%)
    pallas_call x1, Pallas kernels, body(): pl.pallas_call(kernel, out_shape=(out, out), in_specs=[pl.BlockSpec(memor...  25.8 us
    unnamed x8, local copies, waits for them, and re-layouts  5.49 us

profile of v1, /device:TPU:6, one launch (start us, length us, event | category | flops | bytes accessed | tf_op | source)
XLA Modules:
  0.0 31.9 jit_solution(11142002796444456489)
XLA Ops:
  0.6 0.0 copy-start
  0.6 1.2 %copy-done = f32[1,16,128,128]{3,2,1,0:T(8,128)S(1)} copy-done((f32[1,16,128,128]{3,2,1,0:T(8,128)S(1)}, f32[1,16,128,128]{3,2,1,0:T(8,128)}, u32[]{:S(2)}) %copy-start) | copy-done | bytes 1048600
  1.9 0.0 copy-start.1
  1.9 1.2 %copy-done.1 = f32[16,128,128]{2,1,0:T(8,128)S(1)} copy-done((f32[16,128,128]{2,1,0:T(8,128)S(1)}, f32[16,128,128]{2,1,0:T(8,128)}, u32[]{:S(2)}) %copy-start.1) | copy-done | bytes 1048600
  3.1 0.0 copy-start.2
  3.1 1.1 %copy-done.2 = bf16[1408,256]{1,0:T(8,128)(2,1)S(1)} copy-done((bf16[1408,256]{1,0:T(8,128)(2,1)S(1)}, bf16[1408,256]{1,0:T(8,128)(2,1)}, u32[]{:S(2)}) %copy-start.2) | copy-done | bytes 720920
  4.2 25.8 %shard_map.50 = (f32[1,16,128,128]{3,2,1,0:T(8,128)S(1)}, f32[1,16,128,128]{3,2,1,0:T(8,128)S(1)}) custom-call(f32[1,16,128,128]{3,2,1,0:T(8,128)S(1)} %copy-done, f32[16,128,128]{2,1,0:T(8,128)S(1)} %copy-done.1, bf16[1408,256]{1,0:T(8,128)(2,1)S(1)} %copy-done.2), custom_call_target="tpu_custom_call" | custom-call | tf_op jit(solution)/shard_map/pallas_call | solution.py:372
  30.0 1.0 %copy.7 = f32[1,16,128,128]{3,2,1,0:T(8,128)} copy(f32[1,16,128,128]{3,2,1,0:T(8,128)S(1)} %get-tuple-element.4) | data formatting | bytes 2097152
  31.0 1.0 %copy.8 = f32[1,16,128,128]{3,2,1,0:T(8,128)} copy(f32[1,16,128,128]{3,2,1,0:T(8,128)S(1)} %get-tuple-element.5) | data formatting | bytes 2097152
Async XLA Ops:
  0.6 1.2 %copy-start = (f32[1,16,128,128]{3,2,1,0:T(8,128)S(1)}, f32[1,16,128,128]{3,2,1,0:T(8,128)}, u32[]{:S(2)}) copy-start(f32[1,16,128,128]{3,2,1,0:T(8,128)} %a_hbm.1) | copy-start | bytes 3145732
  1.9 1.2 %copy-start.1 = (f32[16,128,128]{2,1,0:T(8,128)S(1)}, f32[16,128,128]{2,1,0:T(8,128)}, u32[]{:S(2)}) copy-start(f32[16,128,128]{2,1,0:T(8,128)} %mob_hbm.1) | copy-start | bytes 3145732
  3.1 1.1 %copy-start.2 = (bf16[1408,256]{1,0:T(8,128)(2,1)S(1)}, bf16[1408,256]{1,0:T(8,128)(2,1)}, u32[]{:S(2)}) copy-start(bf16[1408,256]{1,0:T(8,128)(2,1)} %constant.2.clone.tab_hbm) | copy-start | bytes 2162692

commit v2 on v1

v2 whole, which is shorter than its diff:
```python
import math

import jax
import jax.numpy as jnp
import ml_dtypes
import numpy as np
from jax import lax
from jax.experimental import pallas as pl
from jax.experimental.pallas import tpu as pltpu
from jax.sharding import PartitionSpec as P

KY = 64
KZ = 64
NY = 128
NZ = 128
time_step = 0.05
MESH = pl.DeviceIdType.MESH

FIRST = (7, 6, 5, 4, 0, 3, 2, 1)
SECOND = (7, 6, 5, 4, 3, 2, 1, 0)


def basis_value(node_times, source, point):
    total = 1.0
    for other in range(5):
        if other != source:
            total = total * (point - node_times[other]) / (node_times[source] - node_times[other])
    return total


def picard_table():
    root = math.sqrt(3.0 / 7.0)
    node_times = [0.0, (1.0 - root) / 2.0, 0.5, (1.0 + root) / 2.0, 1.0]
    gauss_points = [-math.sqrt(0.6), 0.0, math.sqrt(0.6)]
    gauss_weights = [5.0 / 9.0, 8.0 / 9.0, 5.0 / 9.0]
    picard_rows = []
    for target in range(1, 5):
        upper = node_times[target]
        row_values = []
        for source in range(5):
            integral = 0.0
            for point, weight in zip(gauss_points, gauss_weights):
                integral = integral + 0.5 * upper * weight * basis_value(
                    node_times, source, 0.5 * upper * (1.0 + point)
                )
            row_values.append(integral)
        picard_rows.append(row_values)
    return picard_rows


def sweep_weights():
    rows = picard_table()
    last = rows[3]
    reach = [time_step * sum(row) for row in rows]
    moments = [sum(last[j] * reach[j - 1] ** k for j in range(1, 5)) for k in range(4)]
    return reach[3], last[0], moments


def dct_rows(count, kept):
    freq = np.arange(kept, dtype=np.float64)[:, None]
    place = np.arange(count, dtype=np.float64)[None, :]
    matrix = np.cos(np.pi * (place + 0.5) * freq / count) * np.sqrt(2.0 / count)
    return np.where(freq == 0, matrix * np.sqrt(0.5), matrix)


def two_parts(matrix):
    high = matrix.astype(ml_dtypes.bfloat16)
    low = (matrix - high.astype(np.float64)).astype(ml_dtypes.bfloat16)
    return high, low


def on_diagonal(block):
    zero = np.zeros_like(block)
    return np.block([[block, zero], [zero, block]])


LA, BA, DS, LS, ROWS = 0, 128, 384, 768, 896


def tables():
    yh, yl = two_parts(dct_rows(NY, KY))
    zh, zl = two_parts(dct_rows(NZ, KZ))
    dh, dl = on_diagonal(zh), on_diagonal(zl)
    parts = [
        np.block([[yh, yh], [yl, yl]]),
        np.concatenate([dh.T, dl.T], axis=1),
        np.concatenate([dh, dh, dl], axis=0),
        np.concatenate([yh.T, yh.T, yl.T, yl.T], axis=1),
    ]
    return np.concatenate(parts, axis=0).astype(ml_dtypes.bfloat16)


def halves(value):
    high = value.astype(jnp.bfloat16)
    low = (value - high.astype(jnp.float32)).astype(jnp.bfloat16)
    return high, low


def mul(left, right):
    return jnp.dot(left, right, preferred_element_type=jnp.float32)


def analyse(first, second, tab):
    high, low = halves(jnp.concatenate([first, second], axis=1))
    out = mul(tab[LA : LA + 128, :], jnp.concatenate([high, low], axis=0))
    high, low = halves(out[:64] + out[64:])
    out = mul(jnp.concatenate([high, low], axis=0), tab[BA : BA + 256, :])
    return (out[:64, :128] + out[64:, :128]) + (out[:64, 128:] + out[64:, 128:])


def synthesise(block, tab):
    high, low = halves(block)
    rows = mul(jnp.concatenate([high, low, high], axis=1), tab[DS : DS + 384, :])
    high, low = halves(rows)
    out = mul(tab[LS : LS + 128, :], jnp.concatenate([high, low, high, low], axis=0))
    return out[:, :128], out[:, 128:]


def kernel(
    a_hbm, mob_hbm, tab_hbm, e_v, n_v,
    a_v, mob_v, tab, f_v, w_v, ap_v, e1_v, ca, cs, cr,
    in_sem, ss, rs, hs, hr,
):
    t = lax.axis_index("tm")
    g = lax.axis_index("gx")
    g_count = lax.axis_size("gx")
    t_count = lax.axis_size("tm")
    has_left, has_right = g > 0, g < g_count - 1
    has_prev, has_next = t > 0, t < t_count - 1
    reach, q0, (s0, s1, s2, s3) = sweep_weights()
    receives = has_prev.astype(jnp.float32)

    a_loads = [
        pltpu.make_async_copy(a_hbm.at[0, pl.ds(4 * c, 4)], a_v.at[pl.ds(1 + 4 * c, 4)], in_sem.at[c]) for c in range(4)
    ]
    mob_loads = [
        pltpu.make_async_copy(mob_hbm.at[pl.ds(4 * c, 4)], mob_v.at[pl.ds(4 * c, 4)], in_sem.at[4 + c])
        for c in range(4)
    ]
    tab_load = pltpu.make_async_copy(tab_hbm, tab, in_sem.at[8])
    for copy in (
        a_loads[1], a_loads[2], a_loads[0], a_loads[3], mob_loads[1], mob_loads[2], tab_load, mob_loads[0], mob_loads[3],
    ):
        copy.start()

    barrier = pltpu.get_barrier_semaphore()
    for present, axis, index in (
        (has_left, "gx", g - 1), (has_right, "gx", g + 1), (has_prev, "tm", t - 1), (has_next, "tm", t + 1),
    ):
        @pl.when(present)
        def _():
            pl.semaphore_signal(barrier, inc=1, device_id={axis: index}, device_id_type=MESH)

    zero = jnp.zeros((128, 128), jnp.float32)

    @pl.when(g == 0)
    def _():
        a_v[0] = zero
        w_v[0] = zero

    @pl.when(g == g_count - 1)
    def _():
        a_v[17] = zero
        w_v[17] = zero

    @pl.when(t == 0)
    def _():
        for stage in range(2):
            for k in range(8):
                cr[stage, k] = jnp.zeros((64, 128), jnp.float32)

    row = lax.broadcasted_iota(jnp.int32, (8, 128), 0)
    lane = lax.broadcasted_iota(jnp.int32, (128, 128), 1)

    def neighbours(ref, p):
        v = ref[p + 1]
        total = ref[p] + ref[p + 2]
        above = pltpu.roll(v, 1, 0)
        below = pltpu.roll(v, 127, 0)
        above = jnp.concatenate([jnp.where(row == 0, 0.0, above[:8]), above[8:]], axis=0)
        below = jnp.concatenate([below[:120], jnp.where(row == 7, 0.0, below[120:])], axis=0)
        total = (total + above) + below
        total = total + jnp.where(lane == 0, 0.0, pltpu.roll(v, 1, 1))
        total = total + jnp.where(lane == 127, 0.0, pltpu.roll(v, 127, 1))
        return total, v

    def send(stage, k):
        return pltpu.make_async_remote_copy(
            src_ref=cs.at[stage, k], dst_ref=cr.at[stage, k], send_sem=ss.at[stage, k], recv_sem=rs.at[stage, k],
            device_id={"tm": t + 1}, device_id_type=MESH,
        )

    def halo(ref, stage, side):
        return pltpu.make_async_remote_copy(
            src_ref=ref.at[1 if side == 0 else 16], dst_ref=ref.at[17 if side == 0 else 0],
            send_sem=hs.at[stage, side], recv_sem=hr.at[stage, side],
            device_id={"gx": g - 1 if side == 0 else g + 1}, device_id_type=MESH,
        )

    def start_halos(ref, stage):
        @pl.when(has_left)
        def _():
            halo(ref, stage, 0).start()

        @pl.when(has_right)
        def _():
            halo(ref, stage, 1).start()

    def take_halos(ref, stage):
        @pl.when(has_right)
        def _():
            halo(ref, stage, 0).wait_recv()

        @pl.when(has_left)
        def _():
            halo(ref, stage, 1).wait_recv()

    def start_send(stage, k):
        @pl.when(has_next)
        def _():
            send(stage, k).start()

    def arrive(stage, k):
        @pl.when(has_prev)
        def _():
            send(stage, k).wait_recv()

    def first_rates(k, slot):
        for i, p in enumerate((k, 15 - k)):
            total, v = neighbours(a_v, p)
            rate = mob_v[p] * (total - v * (5.0 + v * v))
            f_v[p] = rate
            e1_v[slot, i] = v + reach * rate

    def first_coefficients(k, slot):
        cs[0, k] = analyse(e1_v[slot, 0], e1_v[slot, 1], tab)

    def start_coefficients(k):
        ca[k] = receives * analyse(a_v[k + 1], a_v[16 - k], tab)

    a_loads[1].wait()
    a_loads[2].wait()
    mob_loads[1].wait()
    mob_loads[2].wait()
    first_rates(FIRST[0], 0)
    a_loads[0].wait()
    a_loads[3].wait()
    pl.semaphore_wait(
        barrier,
        has_left.astype(jnp.int32) + has_right.astype(jnp.int32) + has_prev.astype(jnp.int32) + has_next.astype(jnp.int32),
    )
    start_halos(a_v, 0)
    tab_load.wait()
    for i in range(1, 9):
        if i == 4:
            mob_loads[0].wait()
            mob_loads[3].wait()
            take_halos(a_v, 0)
        if i < 8:
            first_rates(FIRST[i], i % 2)
        first_coefficients(FIRST[i - 1], (i - 1) % 2)
        if i > 1:
            start_coefficients(FIRST[i - 2])
        start_send(0, FIRST[i - 1])
    start_coefficients(FIRST[7])

    def corrected(k):
        for p, plane in zip((k, 15 - k), synthesise(cr[0, k] - ca[k], tab)):
            start = a_v[p + 1] + plane
            ap_v[p] = start
            w_v[p + 1] = q0 * start + s0 * a_v[p + 1] + s1 * f_v[p]

    def second_values(k):
        for p in (k, 15 - k):
            total, w = neighbours(w_v, p)
            a, f, start = a_v[p + 1], f_v[p], ap_v[p]
            square = a * a
            cubes = (s3 * f + (3.0 * s2) * a) * f + (3.0 * s1) * square
            cubes = cubes * f + s0 * (square * a) + q0 * (start * start * start)
            e_v[0, p] = start + (time_step * mob_v[p]) * ((total - 5.0 * w) - cubes)

    def second_coefficients(k):
        cs[1, k] = analyse(e_v[0, k], e_v[0, 15 - k], tab)

    for first, second, third in (
        (7, None, None), (6, None, None), (5, 7, None), (4, 6, 7), (0, 5, 6), (3, None, 5), (2, 4, None), (1, 3, 4),
        (None, 2, 3), (None, 1, 2), (None, 0, 1), (None, None, 0),
    ):
        if first is not None:
            arrive(0, first)
        if second == 0:
            take_halos(w_v, 1)
        if first is not None:
            corrected(first)
        if second is not None:
            second_values(second)
        if third is not None:
            second_coefficients(third)
        if first == 0:
            start_halos(w_v, 1)
        if third is not None:
            start_send(1, third)

    for k in SECOND:
        arrive(1, k)
        for p, plane in zip((k, 15 - k), synthesise(cr[1, k] - cr[0, k], tab)):
            n_v[0, p] = ap_v[p] + plane

    for stage in range(2):
        @pl.when(has_next)
        def _():
            for k in range(8):
                send(stage, k).wait_send()

        ref = (a_v, w_v)[stage]

        @pl.when(has_left)
        def _():
            halo(ref, stage, 0).wait_send()

        @pl.when(has_right)
        def _():
            halo(ref, stage, 1).wait_send()


def store(e_v, n_v, end_hbm, next_hbm, sem):
    copies = [pltpu.make_async_copy(e_v, end_hbm, sem.at[0]), pltpu.make_async_copy(n_v, next_hbm, sem.at[1])]
    for copy in copies:
        copy.start()
    for copy in copies:
        copy.wait()


def body(start_states, mobility):
    plane = (128, 128)
    f32 = jnp.float32
    shape = start_states.shape
    operands = [
        pltpu.with_memory_space_constraint(x, pltpu.HBM) for x in (start_states, mobility, jnp.asarray(tables()))
    ]
    ends = pl.pallas_call(
        kernel,
        out_shape=[pltpu.VMEM(shape, f32)] * 2,
        in_specs=[pl.BlockSpec(memory_space=pltpu.HBM)] * 3,
        out_specs=[pl.BlockSpec(memory_space=pltpu.VMEM)] * 2,
        scratch_shapes=[
            pltpu.VMEM((18,) + plane, f32),
            pltpu.VMEM((16,) + plane, f32),
            pltpu.VMEM((ROWS, 256), jnp.bfloat16),
            pltpu.VMEM((16,) + plane, f32),
            pltpu.VMEM((18,) + plane, f32),
            pltpu.VMEM((16,) + plane, f32),
            pltpu.VMEM((2, 2) + plane, f32),
            pltpu.VMEM((8, 64, 128), f32),
            pltpu.VMEM((2, 8, 64, 128), f32),
            pltpu.VMEM((2, 8, 64, 128), f32),
            pltpu.SemaphoreType.DMA((9,)),
            pltpu.SemaphoreType.DMA((2, 8)),
            pltpu.SemaphoreType.DMA((2, 8)),
            pltpu.SemaphoreType.DMA((2, 2)),
            pltpu.SemaphoreType.DMA((2, 2)),
        ],
        compiler_params=pltpu.CompilerParams(
            collective_id=0, has_side_effects=True, vmem_limit_bytes=32 * 1024 * 1024
        ),
    )(*operands)
    return tuple(pl.pallas_call(
        store,
        out_shape=[jax.ShapeDtypeStruct(shape, f32)] * 2,
        in_specs=[pl.BlockSpec(memory_space=pltpu.VMEM)] * 2,
        out_specs=[pl.BlockSpec(memory_space=pl.ANY)] * 2,
        scratch_shapes=[pltpu.SemaphoreType.DMA((2,))],
    )(*[pltpu.with_memory_space_constraint(x, pltpu.VMEM) for x in ends]))


def solution(mesh):
    placed = (P("tm", "gx", None, None), P("gx", None, None))
    return jax.shard_map(
        body,
        mesh=mesh,
        in_specs=placed,
        out_specs=(P("tm", "gx", None, None), P("tm", "gx", None, None)),
        check_vma=False,
    )
```

time: 32.1 us -> 25.1 us (0.78)
  the two profiles are of different devices: /device:TPU:6 before, /device:TPU:103 now
where the time goes in v2:
time: 25.1 us; the launch traced here: 25 us
  Pallas kernels  24.3 us (97%)
  between operations  0.64 us (3%)
    pallas_call x1, Pallas kernels, body(): pl.pallas_call(kernel, out_shape=[pltpu.VMEM(shape, f32)] * 2, in_specs=[...  23 us
    pallas_call x1, Pallas kernels, body(): pl.pallas_call(store, out_shape=[jax.ShapeDtypeStruct(shape, f32)] * 2, i...  1.33 us

profile of v2, /device:TPU:103, one launch (start us, length us, event | category | flops | bytes accessed | tf_op | source)
XLA Modules:
  0.0 25.0 jit_solution(14402217558632176419)
XLA Ops:
  0.6 23.0 %shard_map.50 = (f32[1,16,128,128]{3,2,1,0:T(8,128)S(1)}, f32[1,16,128,128]{3,2,1,0:T(8,128)S(1)}) custom-call(f32[1,16,128,128]{3,2,1,0:T(8,128)} %a_hbm.1, f32[16,128,128]{2,1,0:T(8,128)} %mob_hbm.1, bf16[896,256]{1,0:T(8,128)(2,1)} %constant.2.clone.tab_hbm), custom_call_target="tpu_custom_call" | custom-call | tf_op jit(solution)/shard_map/pallas_call | solution.py:341
  23.6 1.3 %shard_map.51 = (f32[1,16,128,128]{3,2,1,0:T(8,128)}, f32[1,16,128,128]{3,2,1,0:T(8,128)}) custom-call(f32[1,16,128,128]{3,2,1,0:T(8,128)S(1)} %get-tuple-element.4.e_v, f32[1,16,128,128]{3,2,1,0:T(8,128)S(1)} %get-tuple-element.5.n_v), custom_call_target="tpu_custom_call" | custom-call | tf_op jit(solution)/shard_map/pallas_call | solution.py:367
